TPU v7x, 32 devices: a whole 2x2x4 slice. The times are simulated.
32 devices in a mesh: rows: 8 (over z, x), cols: 4 (over y, core).
Axes of the slice: x: 2, y: 2, z: 4, core: 2. Of those that a mesh axis runs over, the one named last changes fastest.
Arguments:
- panel_cols: float32 [65536, 256], P(('rows', 'cols')), may hold values from -10000 to 10000, as said below
- trailing: float32 [65536, 1024], P('rows', 'cols'), may hold values from -200000 to 200000
Outputs:
- r_factor: float32 [256, 256], replicated
- r_cross: float32 [256, 1024], P(None, 'cols')
- updated: float32 [65536, 1024], P('rows', 'cols')
Inputs may be any that keep to these rules, and one draw needn't show every extreme that they name: panel_cols has full column rank.
All inputs are finite; a program needn't handle non-finite values.
Results may differ from a plain program's by a relative error of at most 0.0003.
Values sent between devices are 32-bit elements; how exact they have to be, the bound alone decides.
A program may use at most 128 MiB of HBM per device.

v0:
```python
import math

import jax
import jax.numpy as jnp
from jax import lax
from jax.sharding import PartitionSpec as P


def matmul(left, right):
    return jnp.dot(left, right, precision=lax.Precision.HIGHEST)


def lower_factor(gram_sum):
    return jnp.linalg.cholesky(gram_sum)


def lower_inverse(lower):
    identity = jnp.eye(lower.shape[0], dtype=jnp.float32)
    return jax.scipy.linalg.solve_triangular(lower, identity, lower=True)


def local(panel_cols, trailing):
    rows_total = trailing.shape[0] * lax.axis_size("rows")
    shrink = 1.0 / math.sqrt(rows_total)
    row_block = lax.all_gather(panel_cols, "cols", axis=0, tiled=True)
    gram_part = matmul(row_block.T, row_block)
    cross_part = matmul(row_block.T, trailing)
    gram_sum, cross_sum = lax.psum((gram_part, cross_part), "rows")
    lower = lower_factor(gram_sum)
    inverse = lower_inverse(lower)
    coupling = matmul(inverse, cross_sum)
    weights = matmul(inverse.T, coupling)
    updated = trailing - matmul(row_block, weights)
    return (lower.T * shrink, coupling * shrink, updated)


def solution(mesh):
    in_specs = (P(("rows", "cols"), None), P("rows", "cols"))
    out_specs = (P(), P(None, "cols"), P("rows", "cols"))
    return jax.shard_map(local, mesh=mesh, in_specs=in_specs, out_specs=out_specs, check_vma=False)
```

profile of v0, /device:TPU:0, one launch (start us, length us, event | category | flops | bytes accessed | tf_op | source)
XLA Modules:
  0.0 285.4 jit_solution(7421259796326498244)
XLA Ops:
  7.2 0.0 all-gather.2.cloned.1.call-start
  7.2 0.7 all-gather.2.cloned.1.call-update
  7.9 0.0 all-reduce.4.cloned.1.call-start
  7.9 62.6 %all-gather.2.cloned.1.call-done = f32[8192,256]{1,0:T(8,128)} async-done(((f32[2048,256]{1,0:T(8,128)}), f32[8192,256]{1,0:T(8,128)}) %all-gather.2.cloned.1.call-update) | async-done | bytes 8388624 | tf_op jit(solution)/shard_map/all_gather | solution.py:25
  70.6 0.0 copy-start
  70.6 0.0 copy-start.1
  70.6 19.9 %fusion.15 = f32[256,256]{0,1:T(8,128)} fusion(f32[8192,256]{1,0:T(8,128)} %all-gather.2.cloned.1.call-done), kind=kOutput, calls=%fused_computation.39 | convolution fusion | flops 6442450944 | bytes 8650752 | tf_op jit(solution)/shard_map/dot_general | solution.py:10
  90.5 0.0 copy-done
  90.5 0.0 copy-done.1
  90.5 14.7 %fusion.16 = f32[256,256]{1,0:T(8,128)} fusion(f32[8192,256]{1,0:T(8,128)S(1)} %copy-done, f32[8192,256]{1,0:T(8,128)S(1)} %copy-done.1), kind=kOutput, calls=%fused_computation.40 | convolution fusion | flops 6442450944 | bytes 17039360 | tf_op jit(solution)/shard_map/dot_general | solution.py:10
  105.2 0.0 all-reduce.4.cloned.1.call-update
  105.3 8.9 %copy.7 = f32[8192,256]{0,1:T(8,128)} copy(f32[8192,256]{1,0:T(8,128)} %param.3) | data formatting | bytes 16777216 | tf_op args[1]
  114.2 64.0 %all-reduce.4.cloned.1.call-done = (f32[256,256]{0,1:T(8,128)}, f32[256,256]{1,0:T(8,128)}) async-done(((f32[256,256]{0,1:T(8,128)}, f32[256,256]{1,0:T(8,128)}), (f32[256,256]{0,1:T(8,128)}, f32[256,256]{1,0:T(8,128)})) %all-reduce.4.cloned.1.call-update) | async-done | bytes 524304 | tf_op jit(solution)/shard_map/psum | solution.py:28
  178.2 1.1 copy.6
  179.3 1.0 fusion.1
  180.3 11.7 %cholesky.50 = f32[128,128]{1,0:T(8,128)S(1)} custom-call(f32[128,128]{1,0:T(8,128)S(1)} %cholesky.118), custom_call_target="Cholesky" | custom-call | tf_op jit(solution)/shard_map/jit(cholesky)/cholesky | solution.py:14
  192.1 9.8 %custom-call.15 = f32[1,128,128]{1,2,0:T(8,128)S(1)} custom-call(f32[1,128,128]{2,1,0:T(8,128)S(1)} %get-tuple-element.31), custom_call_target="InvertDiagBlocksLowerTriangular" | custom-call | tf_op jit(solution)/shard_map/jit(cholesky)/cholesky | solution.py:14
  201.9 0.2 constant_dynamic-update-slice_fusion.1
  202.1 0.3 convolution_subtract_fusion.1
  202.4 11.7 %cholesky.105 = f32[128,128]{1,0:T(8,128)S(1)} custom-call(f32[128,128]{1,0:T(8,128)S(1)} %convolution_subtract_fusion.1), custom_call_target="Cholesky" | custom-call | tf_op jit(solution)/shard_map/jit(cholesky)/cholesky | solution.py:14
  214.2 0.6 compare_reduce_fusion
  216.2 0.8 copy.8
  217.0 0.1 triangular_solve.44
  217.1 4.0 %while.1 = (s32[]{:T(128)}, f32[256,256]{1,0:T(8,128)S(1)}, s32[2,2]{1,0:T(2,128)S(1)}, f32[2,128,128]{2,1,0:T(8,128)S(1)}, s32[]{:T(128)}) while((s32[]{:T(128)}, f32[256,256]{1,0:T(8,128)S(1)}, s32[2,2]{1,0:T(2,128)S(1)}, f32[2,128,128]{2,1,0:T(8,128)S(1)}, s32[]{:T(128)}) %tuple.30), condition=%wide.while_cond, body=%wide.while_body.sunk | while | flops 2 | bytes 131189 | solution.py:19
  217.1 0.6 fusion.30
  217.7 1.4 bitcast_dynamic-update-slice_fusion.2
  219.1 0.6 fusion.30
  219.6 1.4 bitcast_dynamic-update-slice_fusion.2
  221.0 19.9 %custom-call.16 = f32[2,128,128]{1,2,0:T(8,128)S(1)} custom-call(f32[2,128,128]{2,1,0:T(8,128)S(1)} %get-tuple-element.10), custom_call_target="InvertDiagBlocksLowerTriangular" | custom-call | tf_op jit(solution)/shard_map/jit(_solve_triangular)/triangular_solve | solution.py:19
  241.0 0.3 fusion.5
  241.2 0.3 convolution_subtract_fusion
  241.5 0.3 fusion.8
  241.8 2.0 broadcast_multiply_fusion
  243.9 0.6 fusion.3
  244.5 24.7 %fusion = f32[8192,256]{0,1:T(8,128)} fusion(f32[8192,256]{0,1:T(8,128)} %copy.7, f32[256,256]{1,0:T(8,128)S(1)} %fusion.3, f32[8192,256]{1,0:T(8,128)} %all-gather.2.cloned.1.call-done), kind=kOutput, calls=%fused_computation.3 | convolution fusion | flops 6444548096 | bytes 25427968 | tf_op jit(solution)/shard_map/dot_general | solution.py:10
  269.1 9.0 %copy.9 = f32[8192,256]{1,0:T(8,128)} copy(f32[8192,256]{0,1:T(8,128)} %fusion) | data formatting | bytes 16777216
  (10 shorter events, 0.2 us)
Async XLA Ops:
  7.2 63.4 %all-gather.2.cloned.1.call-start = ((), (), s32[]{:S(2)}) async-start(), calls=%async_computation | async-start | bytes 10485760 | tf_op jit(solution)/shard_map/all_gather | solution.py:25
  7.9 170.4 %all-reduce.4.cloned.1.call-start = ((), (), s32[]{:S(2)}) async-start(), calls=%async_computation.1 | async-start | bytes 1048576 | tf_op jit(solution)/shard_map/psum | solution.py:28
  70.6 19.9 %copy-start = (f32[8192,256]{1,0:T(8,128)S(1)}, f32[8192,256]{1,0:T(8,128)}, u32[]{:S(2)}) copy-start(f32[8192,256]{1,0:T(8,128)} %all-gather.2.cloned.1.call-done) | copy-start | bytes 25165828
  70.6 20.0 %copy-start.1 = (f32[8192,256]{1,0:T(8,128)S(1)}, f32[8192,256]{1,0:T(8,128)}, u32[]{:S(2)}) copy-start(f32[8192,256]{1,0:T(8,128)} %param.3) | copy-start | bytes 25165828
Sparse Core Ops, SparseCore 0:
  9.5 60.9 all-gather.1
  105.4 72.8 all-reduce.3
where the time goes:
time: 291 us; the launch traced here: 285 us
  waiting for transfers between devices  127 us (44%)
  matrix products  63.2 us (22%)
  other arithmetic  54.9 us (19%)
  local copies, waits for them, and re-layouts  23.9 us (8%)
  between operations  15.9 us (5%)
    psum x1, waiting for transfers between devices, local(): gram_sum, cross_sum = lax.psum((gram_part, cross_part), 'rows')  64 us
    all_gather x1, waiting for transfers between devices, local(): row_block = lax.all_gather(panel_cols, 'cols', axis=0, tiled=True)  62.6 us
    dot_general x5, matrix products, matmul(): return jnp.dot(left, right, precision=lax.Precision.HIGHEST)  61.9 us
    another operation x6, other arithmetic, lower_factor(): return jnp.linalg.cholesky(gram_sum)  34 us
    another operation x3, other arithmetic, lower_inverse(): return jax.scipy.linalg.solve_triangular(lower, identity, lower=True)  20 us
    unnamed x7, local copies, waits for them, and re-layouts  18.8 us
  transfers between devices with their start and end apart: 2, of which 2 were waited for; matrix products, arithmetic and copies ran while one was open for 3% of the time, Pallas kernels for 0%

commit v1 on v0

v1 whole, which is shorter than its diff:
```python
import functools
import math

import jax
import jax.numpy as jnp
from jax import lax
from jax.experimental import pallas as pl
from jax.experimental.pallas import tpu as pltpu

MESH = pl.DeviceIdType.MESH
HIGHEST = lax.Precision.HIGHEST
CHUNKS = 8
EARLY = 3
GROUP = 4


def dot(left, right):
    return lax.dot_general(left, right, (((1,), (0,)), ((), ())), precision=HIGHEST, preferred_element_type=jnp.float32)


def dot_t(left, right):
    return lax.dot_general(left, right, (((0,), (0,)), ((), ())), precision=HIGHEST, preferred_element_type=jnp.float32)


def eliminate(a_ref, m_ref, first, last):
    size = a_ref.shape[0]
    sub = lax.broadcasted_iota(jnp.int32, (size, 1), 0)
    lane = lax.broadcasted_iota(jnp.int32, (size, size), 1)
    lane_row = lax.broadcasted_iota(jnp.int32, (1, size), 1)

    def step(index, carry):
        j = index * GROUP
        a = a_ref[...]
        rows = [a_ref[pl.ds(j + t, 1), :] for t in range(GROUP)]
        mrows = [m_ref[pl.ds(j + t, 1), :] for t in range(GROUP)]
        cols = [jnp.sum(jnp.where(lane == j + t, a, 0.0), axis=1, keepdims=True) for t in range(GROUP)]
        head = {
            (t, u): jnp.sum(jnp.where(lane_row == j + u, rows[t], 0.0), axis=1, keepdims=True)
            for t in range(GROUP)
            for u in range(t, GROUP)
        }
        m = m_ref[...]
        for t in range(GROUP):
            inverse = 1.0 / head[t, t]
            factor = jnp.where(sub > j + t, cols[t] * inverse, 0.0)
            ratio = {u: head[t, u] * inverse for u in range(t + 1, GROUP)}
            for u in range(t + 1, GROUP):
                cols[u] = cols[u] - factor * head[t, u]
            for u in range(t + 1, GROUP):
                for v in range(u, GROUP):
                    head[u, v] = head[u, v] - ratio[u] * head[t, v]
            for u in range(t + 1, GROUP):
                rows[u] = rows[u] - ratio[u] * rows[t]
                mrows[u] = mrows[u] - ratio[u] * mrows[t]
            a = a - factor * rows[t]
            m = m - factor * mrows[t]
        a_ref[...] = a
        m_ref[...] = m
        return carry

    lax.fori_loop(first // GROUP, last // GROUP, step, 0)


def scale_rows(a_ref, m_ref):
    size = a_ref.shape[0]
    sub = lax.broadcasted_iota(jnp.int32, (size, size), 0)
    lane = lax.broadcasted_iota(jnp.int32, (size, size), 1)
    a = a_ref[...]
    diagonal = jnp.sum(jnp.where(lane == sub, a, 0.0), axis=1, keepdims=True)
    scale = 1.0 / jnp.sqrt(diagonal)
    return jnp.where(lane >= sub, a * scale, 0.0), m_ref[...] * scale


def unit(size):
    sub = lax.broadcasted_iota(jnp.int32, (size, size), 0)
    lane = lax.broadcasted_iota(jnp.int32, (size, size), 1)
    return jnp.where(lane == sub, 1.0, 0.0).astype(jnp.float32)


def factor_kernel(
    nr, nc,
    panel, trailing, block_out, upper_out, coupling_out, weights_out,
    block, trail, gram, gram_stage, col_stage, gram_sum, cross, cross_stage, cross_sum, work, minv,
    load_sem, out_sem, y_send, y_recv, half_send, half_recv, fwd_send, fwd_recv,
    rs_send, rs_recv, cx_send, cx_recv, ag_send, ag_recv, xrs_send, xrs_recv, xag_send, xag_recv,
):
    me_r, me_c = lax.axis_index("rows"), lax.axis_index("cols")
    depth, width = panel.shape
    half = nc // 2
    side, place = me_c // half, lax.rem(me_c, half)
    across = lax.rem(me_c + half, nc)
    chunk = depth // CHUNKS
    piece = width // nr
    hw = width // 2
    sends = []

    def remote(src, dst, send, recv, where):
        copy = pltpu.make_async_remote_copy(
            src_ref=src, dst_ref=dst, send_sem=send, recv_sem=recv, device_id=where, device_id_type=MESH
        )
        copy.start()
        sends.append(copy)
        return copy

    load_panel = pltpu.make_async_copy(panel, block.at[me_c], load_sem.at[0])
    load_panel.start()
    load_trail = pltpu.make_async_copy(trailing, trail, load_sem.at[1])
    load_trail.start()

    barrier = pltpu.get_barrier_semaphore()
    for d in range(1, nr):
        pl.semaphore_signal(barrier, inc=1, device_id={"rows": lax.rem(me_r + d, nr)}, device_id_type=MESH)
    for d in range(1, nc):
        pl.semaphore_signal(barrier, inc=1, device_id={"cols": lax.rem(me_c + d, nc)}, device_id_type=MESH)
    pl.semaphore_wait(barrier, nr + nc - 2)

    y_copies = []

    def send_across(k):
        rows = pl.ds(k * chunk, chunk)
        y_copies.append(
            remote(panel.at[rows], block.at[me_c, rows], y_send.at[k], y_recv.at[k], {"cols": across})
        )

    for k in range(EARLY):
        send_across(k)
    half_copies = []
    for d in range(1, half):
        peer = side * half + lax.rem(place + d, half)
        half_copies.append(remote(panel, block.at[me_c], half_send.at[d], half_recv.at[d], {"cols": peer}))

    def add_cross(source, first, count):
        def step(i, carry):
            rows = pl.ds(pl.multiple_of(i * chunk, chunk), chunk)
            wide = pl.ds(pl.multiple_of(source * depth + i * chunk, chunk), chunk)
            cross[...] += dot_t(block[source, rows, :], trail[wide, :])
            return carry

        lax.fori_loop(first, first + count, step, 0)

    def store_block(source, first, count, slot):
        rows = pl.ds(first * chunk, count * chunk)
        wide = pl.ds(pl.multiple_of(source * depth + first * chunk, chunk), count * chunk)
        copy = pltpu.make_async_copy(block.at[source, rows], block_out.at[wide], out_sem.at[slot])
        copy.start()
        outs.append(copy)

    outs = []

    load_panel.wait()
    gram[...] = jnp.zeros_like(gram)

    def gram_step(i, carry):
        rows = block[me_c, pl.ds(pl.multiple_of(i * chunk, chunk), chunk), :]
        gram[...] += dot_t(rows, rows)
        return carry

    lax.fori_loop(0, CHUNKS, gram_step, 0)

    def scatter(total, stage, send, recv):
        copies = []
        for d in range(1, nr):
            peer = lax.rem(me_r + d, nr)
            rows = pl.ds(pl.multiple_of(peer * piece, piece), piece)
            copies.append(remote(total.at[rows], stage.at[d], send.at[d], recv.at[d], {"rows": peer}))
        return copies

    def gather(total, send, recv):
        rows = pl.ds(pl.multiple_of(me_r * piece, piece), piece)
        return [
            remote(total.at[rows], total.at[rows], send.at[d], recv.at[d], {"rows": lax.rem(me_r + d, nr)})
            for d in range(1, nr)
        ]

    def arrived(copies):
        for copy in copies:
            copy.wait_recv()

    mine = pl.ds(pl.multiple_of(me_r * piece, piece), piece)

    def summed(total, stage):
        value = total[mine, :]
        for d in range(1, nr):
            value = value + stage[d]
        return value

    gram_rs = scatter(gram, gram_stage, rs_send, rs_recv)
    load_trail.wait()
    cross[...] = jnp.zeros_like(cross)
    add_cross(me_c, 0, CHUNKS)
    store_block(me_c, 0, CHUNKS, 0)
    arrived(gram_rs)
    col_stage[me_c] = summed(gram, gram_stage)
    exchange = [
        remote(col_stage.at[me_c], col_stage.at[me_c], cx_send.at[d], cx_recv.at[d], {"cols": lax.rem(me_c + d, nc)})
        for d in range(1, nc)
    ]
    for k in range(EARLY, CHUNKS):
        send_across(k)
    for d in range(1, half):
        half_copies[d - 1].wait_recv()
        source = side * half + lax.rem(place + half - d, half)
        store_block(source, 0, CHUNKS, d)
        add_cross(source, 0, CHUNKS)
    arrived(exchange)
    value = col_stage[0]
    for c in range(1, nc):
        value = value + col_stage[c]
    gram_sum[mine, :] = value
    gram_ag = gather(gram_sum, ag_send, ag_recv)

    forwards = {}

    def take(k):
        y_copies[k].wait_recv()
        rows = pl.ds(k * chunk, chunk)
        for d in range(1, half):
            peer = side * half + lax.rem(place + d, half)
            slot = (d - 1) * CHUNKS + k
            forwards[d, k] = remote(
                block.at[across, rows], block.at[across, rows], fwd_send.at[slot], fwd_recv.at[slot], {"cols": peer}
            )
        add_cross(across, k, 1)
        store_block(across, k, 1, half + k)

    def take_forward(k):
        for d in range(1, half):
            forwards[d, k].wait_recv()
            source = (1 - side) * half + lax.rem(place + half - d, half)
            add_cross(source, k, 1)
            store_block(source, k, 1, half + CHUNKS * d + k)

    for k in range(EARLY):
        take(k)
        if k:
            take_forward(k - 1)

    def run(first, last, k):
        eliminate(work, minv, first, last)
        if k is not None:
            take(k)
            take_forward(k - 1)

    arrived(gram_ag)
    work[...] = gram_sum[pl.ds(0, hw), pl.ds(0, hw)]
    minv[...] = unit(hw)
    quarter = hw // 4
    run(0, quarter, EARLY)
    run(quarter, 2 * quarter, None)
    run(2 * quarter, 3 * quarter, EARLY + 1)
    run(3 * quarter, hw, None)
    upper1, inverse1 = scale_rows(work, minv)
    cross1 = dot(inverse1, gram_sum[pl.ds(0, hw), pl.ds(hw, hw)])
    upper_out[pl.ds(0, hw), pl.ds(0, hw)] = upper1
    upper_out[pl.ds(0, hw), pl.ds(hw, hw)] = cross1
    upper_out[pl.ds(hw, hw), pl.ds(0, hw)] = jnp.zeros_like(upper1)
    work[...] = gram_sum[pl.ds(hw, hw), pl.ds(hw, hw)] - dot_t(cross1, cross1)
    weights_out[pl.ds(0, hw), pl.ds(0, hw)] = inverse1
    minv[...] = unit(hw)
    run(0, quarter, EARLY + 2)
    run(quarter, 2 * quarter, EARLY + 3)
    run(2 * quarter, 3 * quarter, EARLY + 4)
    take_forward(CHUNKS - 1)
    cross_rs = scatter(cross, cross_stage, xrs_send, xrs_recv)
    run(3 * quarter, hw, None)
    upper2, inverse2 = scale_rows(work, minv)
    upper_out[pl.ds(hw, hw), pl.ds(hw, hw)] = upper2
    inverse1 = weights_out[pl.ds(0, hw), pl.ds(0, hw)]
    corner = -dot(inverse2, dot_t(upper_out[pl.ds(0, hw), pl.ds(hw, hw)], inverse1))
    weights_out[pl.ds(0, hw), pl.ds(hw, hw)] = jnp.zeros_like(inverse1)
    weights_out[pl.ds(hw, hw), pl.ds(0, hw)] = corner
    weights_out[pl.ds(hw, hw), pl.ds(hw, hw)] = inverse2
    arrived(cross_rs)
    cross_sum[mine, :] = summed(cross, cross_stage)
    cross_ag = gather(cross_sum, xag_send, xag_recv)
    for copy in outs:
        copy.wait()
    arrived(cross_ag)
    inverse = weights_out[...]
    coupling = dot(inverse, cross_sum[...])
    coupling_out[...] = coupling
    weights_out[...] = dot_t(inverse, coupling)
    for copy in sends:
        copy.wait_send()


def update_kernel(shrink, block, trailing, upper, coupling, weights, r_factor, r_cross, updated, w_hi, w_lo):
    @pl.when(pl.program_id(0) == 0)
    def _():
        r_factor[...] = upper[...] * shrink
        r_cross[...] = coupling[...] * shrink
        w = weights[...]
        high = w.astype(jnp.bfloat16)
        w_hi[...] = high
        w_lo[...] = (w - high.astype(jnp.float32)).astype(jnp.bfloat16)

    p = block[...]
    p_hi = p.astype(jnp.bfloat16)
    p_lo = (p - p_hi.astype(jnp.float32)).astype(jnp.bfloat16)

    def mul(left, right):
        return jnp.dot(left, right, preferred_element_type=jnp.float32)

    product = mul(p_hi, w_hi[...]) + (mul(p_lo, w_hi[...]) + mul(p_hi, w_lo[...]))
    updated[...] = trailing[...] - product


def local(nr, nc, panel_cols, trailing):
    depth, width = panel_cols.shape
    rows, cols = trailing.shape
    half = nc // 2
    piece = width // nr
    f32 = jnp.float32
    square = jax.ShapeDtypeStruct((width, width), f32)
    tall = jax.ShapeDtypeStruct((width, cols), f32)
    dma = pltpu.SemaphoreType.DMA
    vmem = pl.BlockSpec(memory_space=pltpu.VMEM)
    hbm = pl.BlockSpec(memory_space=pl.ANY)
    block, upper, coupling, weights = pl.pallas_call(
        functools.partial(factor_kernel, nr, nc),
        out_shape=(jax.ShapeDtypeStruct((rows, width), f32), square, tall, tall),
        in_specs=[hbm, hbm],
        out_specs=(hbm, vmem, vmem, vmem),
        scratch_shapes=[
            pltpu.VMEM((nc, depth, width), f32),
            pltpu.VMEM((rows, cols), f32),
            pltpu.VMEM((width, width), f32),
            pltpu.VMEM((nr, piece, width), f32),
            pltpu.VMEM((nc, piece, width), f32),
            pltpu.VMEM((width, width), f32),
            pltpu.VMEM((width, cols), f32),
            pltpu.VMEM((nr, piece, cols), f32),
            pltpu.VMEM((width, cols), f32),
            pltpu.VMEM((width // 2, width // 2), f32),
            pltpu.VMEM((width // 2, width // 2), f32),
            dma((2,)),
            dma((half + CHUNKS * half,)),
            dma((CHUNKS,)), dma((CHUNKS,)),
            dma((half,)), dma((half,)),
            dma((CHUNKS * half,)), dma((CHUNKS * half,)),
            dma((nr,)), dma((nr,)),
            dma((nc,)), dma((nc,)),
            dma((nr,)), dma((nr,)),
            dma((nr,)), dma((nr,)),
            dma((nr,)), dma((nr,)),
        ],
        compiler_params=pltpu.CompilerParams(
            collective_id=0, has_side_effects=True, vmem_limit_bytes=40 * 1024 * 1024
        ),
        name="factor",
    )(panel_cols, trailing)

    tile = rows // 8
    fixed = lambda i: (0, 0)
    shrink = 1.0 / math.sqrt(rows * nr)
    r_factor, r_cross, updated = pl.pallas_call(
        functools.partial(update_kernel, shrink),
        grid=(rows // tile,),
        out_shape=(square, tall, jax.ShapeDtypeStruct((rows, cols), f32)),
        in_specs=[
            pl.BlockSpec((tile, width), lambda i: (i, 0)),
            pl.BlockSpec((tile, cols), lambda i: (i, 0)),
            pl.BlockSpec((width, width), fixed),
            pl.BlockSpec((width, cols), fixed),
            pl.BlockSpec((width, cols), fixed),
        ],
        out_specs=(
            pl.BlockSpec((width, width), fixed),
            pl.BlockSpec((width, cols), fixed),
            pl.BlockSpec((tile, cols), lambda i: (i, 0)),
        ),
        scratch_shapes=[pltpu.VMEM((width, cols), jnp.bfloat16)] * 2,
        name="update",
    )(block, trailing, upper, coupling, weights)
    return r_factor, r_cross, updated


def solution(mesh):
    P = jax.sharding.PartitionSpec
    body = functools.partial(local, mesh.shape["rows"], mesh.shape["cols"])
    in_specs = (P(("rows", "cols"), None), P("rows", "cols"))
    out_specs = (P(), P(None, "cols"), P("rows", "cols"))
    return jax.shard_map(body, mesh=mesh, in_specs=in_specs, out_specs=out_specs, check_vma=False)
```

time: 291 us -> 92.5 us (0.32); the launches traced: 285 us -> 92.2 us
  waiting for transfers between devices: 127 us -> 0 us
  Pallas kernels: 0 us -> 84.6 us
  matrix products: 63.2 us -> 0 us
  other arithmetic: 54.9 us -> 0 us
  local copies, waits for them, and re-layouts: 23.9 us -> 6.96 us
  between operations: 15.9 us -> 0.66 us
    pallas_call x0 -> x2, Pallas kernels: none -> 84.6 us  [the longest x1 71.8 us: local(): pl.pallas_call(functools.partial(factor_kernel, nr, nc), out_shape=(jax.S...]
    psum x1 -> x0, waiting for transfers between devices: 64 us -> none  [local(): gram_sum, cross_sum = lax.psum((gram_part, cross_part), 'rows')]
    all_gather x1 -> x0, waiting for transfers between devices: 62.6 us -> none  [local(): row_block = lax.all_gather(panel_cols, 'cols', axis=0, tiled=True)]
    dot_general x5 -> x0, matrix products: 61.9 us -> none  [matmul(): return jnp.dot(left, right, precision=lax.Precision.HIGHEST)]
    another operation x9 -> x0, other arithmetic: 53.9 us -> none  [the longest x6 34 us: lower_factor(): return jnp.linalg.cholesky(gram_sum)]
    unnamed x7 -> x10, local copies, waits for them, and re-layouts: 18.8 us -> 6.96 us
    another operation x9 -> x0, local copies, waits for them, and re-layouts: 4.02 us -> none
  transfers between devices with their start and end apart: 2 -> 0, of which waited for: 2 -> 0; matrix products, arithmetic and copies ran while one was open for 3% -> 0% of each run, Pallas kernels for 0% -> 0%
where the time goes in v1:
time: 92.5 us; the launch traced here: 92.2 us
  Pallas kernels  84.6 us (91%)
  local copies, waits for them, and re-layouts  6.96 us (8%)
    pallas_call x1, Pallas kernels, local(): pl.pallas_call(functools.partial(factor_kernel, nr, nc), out_shape=(jax.S...  71.8 us
    pallas_call x1, Pallas kernels, local(): pl.pallas_call(functools.partial(update_kernel, shrink), grid=(rows // ti...  12.8 us
    unnamed x10, local copies, waits for them, and re-layouts  6.96 us

profile of v1, /device:TPU:0, one launch (start us, length us, event | category | flops | bytes accessed | tf_op | source)
XLA Modules:
  0.0 92.2 jit_solution(15131175214129723996)
XLA Ops:
  0.6 0.0 copy-start.1
  0.6 1.6 %copy-done.1 = f32[2048,256]{1,0:T(8,128)S(1)} copy-done((f32[2048,256]{1,0:T(8,128)S(1)}, f32[2048,256]{1,0:T(8,128)}, u32[]{:S(2)}) %copy-start.1) | copy-done | bytes 2097176
  2.2 71.8 %factor.1 = (f32[8192,256]{1,0:T(8,128)S(1)}, f32[256,256]{1,0:T(8,128)S(1)}, f32[256,256]{1,0:T(8,128)S(1)}, f32[256,256]{1,0:T(8,128)S(1)}) custom-call(f32[2048,256]{1,0:T(8,128)S(1)} %copy-done.1, f32[8192,256]{1,0:T(8,128)} %trailing.3), custom_call_target="tpu_custom_call" | custom-call | tf_op jit(solution)/shard_map/factor/pallas_call | solution.py:319
  74.0 0.0 copy-start
  74.0 3.2 %copy-done = f32[8192,256]{1,0:T(8,128)} copy-done((f32[8192,256]{1,0:T(8,128)}, f32[8192,256]{1,0:T(8,128)S(1)}, u32[]{:S(2)}) %copy-start) | copy-done | bytes 8388632
  77.2 0.0 copy-start.2
  77.2 0.7 copy-done.2
  78.0 0.0 copy-start.3
  78.0 0.7 copy-done.3
  78.7 0.0 copy-start.4
  78.7 0.7 copy-done.4
  79.4 12.8 %update.1 = (f32[256,256]{1,0:T(8,128)}, f32[256,256]{1,0:T(8,128)}, f32[8192,256]{1,0:T(8,128)}) custom-call(f32[8192,256]{1,0:T(8,128)} %copy-done, f32[8192,256]{1,0:T(8,128)} %trailing.3, f32[256,256]{1,0:T(8,128)} %copy-done.2, f32[256,256]{1,0:T(8,128)} %copy-done.3, f32[256,256]{1,0:T(8,128)} %copy-done.4), custom_call_target="tpu_custom_call" | custom-call | tf_op jit(solution)/shard_map/update/pallas_call | solution.py:356
Async XLA Ops:
  0.6 1.6 %copy-start.1 = (f32[2048,256]{1,0:T(8,128)S(1)}, f32[2048,256]{1,0:T(8,128)}, u32[]{:S(2)}) copy-start(f32[2048,256]{1,0:T(8,128)} %panel.1) | copy-start | bytes 6291460
  74.0 3.2 %copy-start = (f32[8192,256]{1,0:T(8,128)}, f32[8192,256]{1,0:T(8,128)S(1)}, u32[]{:S(2)}) copy-start(f32[8192,256]{1,0:T(8,128)S(1)} %get-tuple-element.7.block) | copy-start | bytes 25165828
  77.2 0.7 copy-start.2
  78.0 0.7 copy-start.3
  78.7 0.7 copy-start.4

commit v2 on v1

--- a/solution.py
+++ b/solution.py
@@ -12,6 +12,7 @@
 CHUNKS = 8
 EARLY = 3
 GROUP = 4
+TILES = 16
 
 
 def dot(left, right):
@@ -79,9 +80,9 @@
 
 def factor_kernel(
     nr, nc,
-    panel, trailing, block_out, upper_out, coupling_out, weights_out,
-    block, trail, gram, gram_stage, col_stage, gram_sum, cross, cross_stage, cross_sum, work, minv,
-    load_sem, out_sem, y_send, y_recv, half_send, half_recv, fwd_send, fwd_recv,
+    panel, trailing, block, trail, upper_out, coupling_out, weights_out,
+    gram, gram_stage, col_stage, gram_sum, cross, cross_stage, cross_sum, work, minv,
+    load_sem, y_send, y_recv, half_send, half_recv, fwd_send, fwd_recv,
     rs_send, rs_recv, cx_send, cx_recv, ag_send, ag_recv, xrs_send, xrs_recv, xag_send, xag_recv,
 ):
     me_r, me_c = lax.axis_index("rows"), lax.axis_index("cols")
@@ -138,15 +139,6 @@
 
         lax.fori_loop(first, first + count, step, 0)
 
-    def store_block(source, first, count, slot):
-        rows = pl.ds(first * chunk, count * chunk)
-        wide = pl.ds(pl.multiple_of(source * depth + first * chunk, chunk), count * chunk)
-        copy = pltpu.make_async_copy(block.at[source, rows], block_out.at[wide], out_sem.at[slot])
-        copy.start()
-        outs.append(copy)
-
-    outs = []
-
     load_panel.wait()
     gram[...] = jnp.zeros_like(gram)
 
@@ -188,7 +180,6 @@
     load_trail.wait()
     cross[...] = jnp.zeros_like(cross)
     add_cross(me_c, 0, CHUNKS)
-    store_block(me_c, 0, CHUNKS, 0)
     arrived(gram_rs)
     col_stage[me_c] = summed(gram, gram_stage)
     exchange = [
@@ -200,7 +191,6 @@
     for d in range(1, half):
         half_copies[d - 1].wait_recv()
         source = side * half + lax.rem(place + half - d, half)
-        store_block(source, 0, CHUNKS, d)
         add_cross(source, 0, CHUNKS)
     arrived(exchange)
     value = col_stage[0]
@@ -221,14 +211,12 @@
                 block.at[across, rows], block.at[across, rows], fwd_send.at[slot], fwd_recv.at[slot], {"cols": peer}
             )
         add_cross(across, k, 1)
-        store_block(across, k, 1, half + k)
 
     def take_forward(k):
         for d in range(1, half):
             forwards[d, k].wait_recv()
             source = (1 - side) * half + lax.rem(place + half - d, half)
             add_cross(source, k, 1)
-            store_block(source, k, 1, half + CHUNKS * d + k)
 
     for k in range(EARLY):
         take(k)
@@ -273,8 +261,6 @@
     arrived(cross_rs)
     cross_sum[mine, :] = summed(cross, cross_stage)
     cross_ag = gather(cross_sum, xag_send, xag_recv)
-    for copy in outs:
-        copy.wait()
     arrived(cross_ag)
     inverse = weights_out[...]
     coupling = dot(inverse, cross_sum[...])
@@ -284,25 +270,48 @@
         copy.wait_send()
 
 
-def update_kernel(shrink, block, trailing, upper, coupling, weights, r_factor, r_cross, updated, w_hi, w_lo):
-    @pl.when(pl.program_id(0) == 0)
-    def _():
-        r_factor[...] = upper[...] * shrink
-        r_cross[...] = coupling[...] * shrink
-        w = weights[...]
-        high = w.astype(jnp.bfloat16)
-        w_hi[...] = high
-        w_lo[...] = (w - high.astype(jnp.float32)).astype(jnp.bfloat16)
-
-    p = block[...]
-    p_hi = p.astype(jnp.bfloat16)
-    p_lo = (p - p_hi.astype(jnp.float32)).astype(jnp.bfloat16)
+def update_kernel(
+    shrink, block, trailing, upper, coupling, weights, r_factor, r_cross, updated,
+    small, w_hi, w_lo, out, small_sem, out_sem,
+):
+    small[0] = upper[...] * shrink
+    small[1] = coupling[...] * shrink
+    copies = [
+        pltpu.make_async_copy(small.at[0], r_factor, small_sem.at[0]),
+        pltpu.make_async_copy(small.at[1], r_cross, small_sem.at[1]),
+    ]
+    for copy in copies:
+        copy.start()
+    w = weights[...]
+    high = w.astype(jnp.bfloat16)
+    w_hi[...] = high
+    w_lo[...] = (w - high.astype(jnp.float32)).astype(jnp.bfloat16)
+    tile = out.shape[0] // TILES
 
     def mul(left, right):
         return jnp.dot(left, right, preferred_element_type=jnp.float32)
 
-    product = mul(p_hi, w_hi[...]) + (mul(p_lo, w_hi[...]) + mul(p_hi, w_lo[...]))
-    updated[...] = trailing[...] - product
+    def window(i):
+        return pl.ds(pl.multiple_of(i * tile, tile), tile)
+
+    def store(i):
+        return pltpu.make_async_copy(out.at[window(i)], updated.at[window(i)], out_sem.at[i])
+
+    def step(i, carry):
+        rows = window(i)
+        p = block[rows, :]
+        p_hi = p.astype(jnp.bfloat16)
+        p_lo = (p - p_hi.astype(jnp.float32)).astype(jnp.bfloat16)
+        product = mul(p_hi, w_hi[...]) + (mul(p_lo, w_hi[...]) + mul(p_hi, w_lo[...]))
+        out[rows, :] = trailing[rows, :] - product
+        store(i).start()
+        return carry
+
+    lax.fori_loop(0, TILES, step, 0)
+    for i in range(TILES):
+        store(i).wait()
+    for copy in copies:
+        copy.wait()
 
 
 def local(nr, nc, panel_cols, trailing):
@@ -315,15 +324,13 @@
     tall = jax.ShapeDtypeStruct((width, cols), f32)
     dma = pltpu.SemaphoreType.DMA
     vmem = pl.BlockSpec(memory_space=pltpu.VMEM)
-    hbm = pl.BlockSpec(memory_space=pl.ANY)
-    block, upper, coupling, weights = pl.pallas_call(
+    hbm = pl.BlockSpec(memory_space=pltpu.HBM)
+    block, trail, upper, coupling, weights = pl.pallas_call(
         functools.partial(factor_kernel, nr, nc),
-        out_shape=(jax.ShapeDtypeStruct((rows, width), f32), square, tall, tall),
+        out_shape=(jax.ShapeDtypeStruct((nc, depth, width), f32), jax.ShapeDtypeStruct((rows, cols), f32), square, tall, tall),
         in_specs=[hbm, hbm],
-        out_specs=(hbm, vmem, vmem, vmem),
+        out_specs=(vmem,) * 5,
         scratch_shapes=[
-            pltpu.VMEM((nc, depth, width), f32),
-            pltpu.VMEM((rows, cols), f32),
             pltpu.VMEM((width, width), f32),
             pltpu.VMEM((nr, piece, width), f32),
             pltpu.VMEM((nc, piece, width), f32),
@@ -334,7 +341,6 @@
             pltpu.VMEM((width // 2, width // 2), f32),
             pltpu.VMEM((width // 2, width // 2), f32),
             dma((2,)),
-            dma((half + CHUNKS * half,)),
             dma((CHUNKS,)), dma((CHUNKS,)),
             dma((half,)), dma((half,)),
             dma((CHUNKS * half,)), dma((CHUNKS * half,)),
@@ -345,33 +351,28 @@
             dma((nr,)), dma((nr,)),
         ],
         compiler_params=pltpu.CompilerParams(
-            collective_id=0, has_side_effects=True, vmem_limit_bytes=40 * 1024 * 1024
+            collective_id=0, has_side_effects=True, vmem_limit_bytes=20 * 1024 * 1024
         ),
         name="factor",
-    )(panel_cols, trailing)
-
-    tile = rows // 8
-    fixed = lambda i: (0, 0)
+    )(*(pltpu.with_memory_space_constraint(x, pltpu.HBM) for x in (panel_cols, trailing)))
+
     shrink = 1.0 / math.sqrt(rows * nr)
     r_factor, r_cross, updated = pl.pallas_call(
         functools.partial(update_kernel, shrink),
-        grid=(rows // tile,),
         out_shape=(square, tall, jax.ShapeDtypeStruct((rows, cols), f32)),
-        in_specs=[
-            pl.BlockSpec((tile, width), lambda i: (i, 0)),
-            pl.BlockSpec((tile, cols), lambda i: (i, 0)),
-            pl.BlockSpec((width, width), fixed),
-            pl.BlockSpec((width, cols), fixed),
-            pl.BlockSpec((width, cols), fixed),
+        in_specs=[vmem] * 5,
+        out_specs=(hbm,) * 3,
+        scratch_shapes=[
+            pltpu.VMEM((2, width, cols), f32),
+            pltpu.VMEM((width, cols), jnp.bfloat16),
+            pltpu.VMEM((width, cols), jnp.bfloat16),
+            pltpu.VMEM((rows, cols), f32),
+            dma((2,)),
+            dma((TILES,)),
         ],
-        out_specs=(
-            pl.BlockSpec((width, width), fixed),
-            pl.BlockSpec((width, cols), fixed),
-            pl.BlockSpec((tile, cols), lambda i: (i, 0)),
-        ),
-        scratch_shapes=[pltpu.VMEM((width, cols), jnp.bfloat16)] * 2,
+        compiler_params=pltpu.CompilerParams(vmem_limit_bytes=24 * 1024 * 1024),
         name="update",
-    )(block, trailing, upper, coupling, weights)
+    )(block.reshape(rows, width), trail, upper, coupling, weights)
     return r_factor, r_cross, updated
 
 

time: 92.5 us -> 79.5 us (0.86)
  local copies, waits for them, and re-layouts: 6.96 us -> 0 us
  Pallas kernels: 84.6 us -> 78.7 us
    unnamed x10 -> x0, local copies, waits for them, and re-layouts: 6.96 us -> none
    pallas_call x1, Pallas kernels: 12.8 us -> 7.03 us  [local(): pl.pallas_call(functools.partial(update_kernel, shrink), out_shape=(squar...]
where the time goes in v2:
time: 79.5 us; the launch traced here: 79.4 us
  Pallas kernels  78.7 us (99%)
    pallas_call x1, Pallas kernels, local(): pl.pallas_call(functools.partial(factor_kernel, nr, nc), out_shape=(jax.S...  71.7 us
    pallas_call x1, Pallas kernels, local(): pl.pallas_call(functools.partial(update_kernel, shrink), out_shape=(squar...  7.03 us

profile of v2, /device:TPU:0, one launch (start us, length us, event | category | flops | bytes accessed | tf_op | source)
XLA Modules:
  0.0 79.4 jit_solution(12835618153138509232)
XLA Ops:
  0.6 71.7 %factor.1 = (f32[4,2048,256]{2,1,0:T(8,128)S(1)}, f32[8192,256]{1,0:T(8,128)S(1)}, f32[256,256]{1,0:T(8,128)S(1)}, f32[256,256]{1,0:T(8,128)S(1)}, f32[256,256]{1,0:T(8,128)S(1)}) custom-call(f32[2048,256]{1,0:T(8,128)} %panel.1, f32[8192,256]{1,0:T(8,128)} %trailing.1), custom_call_target="tpu_custom_call" | custom-call | tf_op jit(solution)/shard_map/factor/pallas_call | solution.py:328
  72.3 7.0 %update.1 = (f32[256,256]{1,0:T(8,128)}, f32[256,256]{1,0:T(8,128)}, f32[8192,256]{1,0:T(8,128)}) custom-call(f32[8192,256]{1,0:T(8,128)S(1)} %bitcast.1, f32[8192,256]{1,0:T(8,128)S(1)} %get-tuple-element.9.trailing, f32[256,256]{1,0:T(8,128)S(1)} %get-tuple-element.10.upper, f32[256,256]{1,0:T(8,128)S(1)} %get-tuple-element.11.coupling, ...), custom_call_target="tpu_custom_call" | custom-call | tf_op jit(solution)/shard_map/update/pallas_call | solution.py:360

commit v3 on v2

--- a/solution.py
+++ b/solution.py
@@ -11,6 +11,7 @@
 HIGHEST = lax.Precision.HIGHEST
 CHUNKS = 8
 EARLY = 3
+MORE = (1, 1, 1, 0, 1, 0, 1, 0)
 GROUP = 4
 TILES = 16
 
@@ -81,7 +82,7 @@
 def factor_kernel(
     nr, nc,
     panel, trailing, block, trail, upper_out, coupling_out, weights_out,
-    gram, gram_stage, col_stage, gram_sum, cross, cross_stage, cross_sum, work, minv,
+    gram, gram_stage, col_stage, gram_sum, cross, cross_stage, cross_sum, work, minv, inv,
     load_sem, y_send, y_recv, half_send, half_recv, fwd_send, fwd_recv,
     rs_send, rs_recv, cx_send, cx_recv, ag_send, ag_recv, xrs_send, xrs_recv, xag_send, xag_recv,
 ):
@@ -92,6 +93,11 @@
     across = lax.rem(me_c + half, nc)
     chunk = depth // CHUNKS
     piece = width // nr
+    groups = cross.shape[0]
+    per_group = CHUNKS // groups
+    deep = depth // per_group
+    wide = width // groups
+    cross_piece = wide // nr
     hw = width // 2
     sends = []
 
@@ -115,12 +121,15 @@
         pl.semaphore_signal(barrier, inc=1, device_id={"cols": lax.rem(me_c + d, nc)}, device_id_type=MESH)
     pl.semaphore_wait(barrier, nr + nc - 2)
 
+    def item(k):
+        return pl.ds((k % per_group) * deep, deep), pl.ds((k // per_group) * wide, wide)
+
     y_copies = []
 
     def send_across(k):
-        rows = pl.ds(k * chunk, chunk)
+        rows, lanes = item(k)
         y_copies.append(
-            remote(panel.at[rows], block.at[me_c, rows], y_send.at[k], y_recv.at[k], {"cols": across})
+            remote(panel.at[rows, lanes], block.at[me_c, rows, lanes], y_send.at[k], y_recv.at[k], {"cols": across})
         )
 
     for k in range(EARLY):
@@ -130,14 +139,21 @@
         peer = side * half + lax.rem(place + d, half)
         half_copies.append(remote(panel, block.at[me_c], half_send.at[d], half_recv.at[d], {"cols": peer}))
 
-    def add_cross(source, first, count):
+    def add_cross(source):
         def step(i, carry):
             rows = pl.ds(pl.multiple_of(i * chunk, chunk), chunk)
-            wide = pl.ds(pl.multiple_of(source * depth + i * chunk, chunk), chunk)
-            cross[...] += dot_t(block[source, rows, :], trail[wide, :])
+            long = pl.ds(pl.multiple_of(source * depth + i * chunk, chunk), chunk)
+            product = dot_t(block[source, rows, :], trail[long, :])
+            for g in range(groups):
+                cross[g] += product[g * wide : (g + 1) * wide, :]
             return carry
 
-        lax.fori_loop(first, first + count, step, 0)
+        lax.fori_loop(0, CHUNKS, step, 0)
+
+    def add_item(source, k):
+        rows, lanes = item(k)
+        long = pl.ds(pl.multiple_of(source * depth + (k % per_group) * deep, deep), deep)
+        cross[k // per_group] += dot_t(block[source, rows, lanes], trail[long, :])
 
     load_panel.wait()
     gram[...] = jnp.zeros_like(gram)
@@ -149,7 +165,7 @@
 
     lax.fori_loop(0, CHUNKS, gram_step, 0)
 
-    def scatter(total, stage, send, recv):
+    def scatter(total, stage, send, recv, piece=piece):
         copies = []
         for d in range(1, nr):
             peer = lax.rem(me_r + d, nr)
@@ -157,7 +173,7 @@
             copies.append(remote(total.at[rows], stage.at[d], send.at[d], recv.at[d], {"rows": peer}))
         return copies
 
-    def gather(total, send, recv):
+    def gather(total, send, recv, piece=piece):
         rows = pl.ds(pl.multiple_of(me_r * piece, piece), piece)
         return [
             remote(total.at[rows], total.at[rows], send.at[d], recv.at[d], {"rows": lax.rem(me_r + d, nr)})
@@ -169,8 +185,9 @@
             copy.wait_recv()
 
     mine = pl.ds(pl.multiple_of(me_r * piece, piece), piece)
-
-    def summed(total, stage):
+    cross_mine = pl.ds(pl.multiple_of(me_r * cross_piece, cross_piece), cross_piece)
+
+    def summed(total, stage, mine=mine):
         value = total[mine, :]
         for d in range(1, nr):
             value = value + stage[d]
@@ -179,7 +196,7 @@
     gram_rs = scatter(gram, gram_stage, rs_send, rs_recv)
     load_trail.wait()
     cross[...] = jnp.zeros_like(cross)
-    add_cross(me_c, 0, CHUNKS)
+    add_cross(me_c)
     arrived(gram_rs)
     col_stage[me_c] = summed(gram, gram_stage)
     exchange = [
@@ -191,7 +208,7 @@
     for d in range(1, half):
         half_copies[d - 1].wait_recv()
         source = side * half + lax.rem(place + half - d, half)
-        add_cross(source, 0, CHUNKS)
+        add_cross(source)
     arrived(exchange)
     value = col_stage[0]
     for c in range(1, nc):
@@ -203,67 +220,80 @@
 
     def take(k):
         y_copies[k].wait_recv()
-        rows = pl.ds(k * chunk, chunk)
+        rows, lanes = item(k)
         for d in range(1, half):
             peer = side * half + lax.rem(place + d, half)
             slot = (d - 1) * CHUNKS + k
-            forwards[d, k] = remote(
-                block.at[across, rows], block.at[across, rows], fwd_send.at[slot], fwd_recv.at[slot], {"cols": peer}
-            )
-        add_cross(across, k, 1)
+            part = block.at[across, rows, lanes]
+            forwards[d, k] = remote(part, part, fwd_send.at[slot], fwd_recv.at[slot], {"cols": peer})
+        add_item(across, k)
 
     def take_forward(k):
         for d in range(1, half):
             forwards[d, k].wait_recv()
             source = (1 - side) * half + lax.rem(place + half - d, half)
-            add_cross(source, k, 1)
-
-    for k in range(EARLY):
-        take(k)
-        if k:
-            take_forward(k - 1)
-
-    def run(first, last, k):
+            add_item(source, k)
+
+    cross_rs, cross_ag = {}, {}
+
+    def start_cross(g):
+        cross_rs[g] = scatter(cross.at[g], cross_stage.at[g], xrs_send.at[g], xrs_recv.at[g], cross_piece)
+
+    def share_cross(g):
+        arrived(cross_rs[g])
+        cross_sum[g, cross_mine, :] = summed(cross.at[g], cross_stage.at[g], cross_mine)
+        cross_ag[g] = gather(cross_sum.at[g], xag_send.at[g], xag_recv.at[g], cross_piece)
+
+    pending = []
+    for k in range(CHUNKS):
+        pending.append([functools.partial(take, k)] + ([functools.partial(take_forward, k - 1)] if k % per_group else []))
+        if k % per_group == per_group - 1:
+            pending[-1].append(functools.partial(take_forward, k))
+            pending[-1].append(functools.partial(start_cross, k // per_group))
+    for g in range(groups - 1):
+        pending[(g + 1) * per_group + 1].append(functools.partial(share_cross, g))
+
+    def advance():
+        for task in pending.pop(0):
+            task()
+
+    def run(first, last, more):
         eliminate(work, minv, first, last)
-        if k is not None:
-            take(k)
-            take_forward(k - 1)
-
+        if more:
+            advance()
+
+    for _ in range(EARLY):
+        advance()
     arrived(gram_ag)
     work[...] = gram_sum[pl.ds(0, hw), pl.ds(0, hw)]
     minv[...] = unit(hw)
     quarter = hw // 4
-    run(0, quarter, EARLY)
-    run(quarter, 2 * quarter, None)
-    run(2 * quarter, 3 * quarter, EARLY + 1)
-    run(3 * quarter, hw, None)
+    for q in range(4):
+        run(q * quarter, (q + 1) * quarter, MORE[q])
     upper1, inverse1 = scale_rows(work, minv)
     cross1 = dot(inverse1, gram_sum[pl.ds(0, hw), pl.ds(hw, hw)])
     upper_out[pl.ds(0, hw), pl.ds(0, hw)] = upper1
     upper_out[pl.ds(0, hw), pl.ds(hw, hw)] = cross1
     upper_out[pl.ds(hw, hw), pl.ds(0, hw)] = jnp.zeros_like(upper1)
     work[...] = gram_sum[pl.ds(hw, hw), pl.ds(hw, hw)] - dot_t(cross1, cross1)
-    weights_out[pl.ds(0, hw), pl.ds(0, hw)] = inverse1
+    inv[pl.ds(0, hw), pl.ds(0, hw)] = inverse1
     minv[...] = unit(hw)
-    run(0, quarter, EARLY + 2)
-    run(quarter, 2 * quarter, EARLY + 3)
-    run(2 * quarter, 3 * quarter, EARLY + 4)
-    take_forward(CHUNKS - 1)
-    cross_rs = scatter(cross, cross_stage, xrs_send, xrs_recv)
-    run(3 * quarter, hw, None)
+    for q in range(4):
+        run(q * quarter, (q + 1) * quarter, MORE[4 + q])
     upper2, inverse2 = scale_rows(work, minv)
     upper_out[pl.ds(hw, hw), pl.ds(hw, hw)] = upper2
-    inverse1 = weights_out[pl.ds(0, hw), pl.ds(0, hw)]
+    inverse1 = inv[pl.ds(0, hw), pl.ds(0, hw)]
     corner = -dot(inverse2, dot_t(upper_out[pl.ds(0, hw), pl.ds(hw, hw)], inverse1))
-    weights_out[pl.ds(0, hw), pl.ds(hw, hw)] = jnp.zeros_like(inverse1)
-    weights_out[pl.ds(hw, hw), pl.ds(0, hw)] = corner
-    weights_out[pl.ds(hw, hw), pl.ds(hw, hw)] = inverse2
-    arrived(cross_rs)
-    cross_sum[mine, :] = summed(cross, cross_stage)
-    cross_ag = gather(cross_sum, xag_send, xag_recv)
-    arrived(cross_ag)
-    inverse = weights_out[...]
-    coupling = dot(inverse, cross_sum[...])
+    inv[pl.ds(0, hw), pl.ds(hw, hw)] = jnp.zeros_like(inverse1)
+    inv[pl.ds(hw, hw), pl.ds(0, hw)] = corner
+    inv[pl.ds(hw, hw), pl.ds(hw, hw)] = inverse2
+    while pending:
+        advance()
+    share_cross(groups - 1)
+    for g in range(groups):
+        arrived(cross_ag[g])
+    inverse = inv[...]
+    coupling = dot(inverse, jnp.concatenate([cross_sum[g] for g in range(groups)], axis=0))
     coupling_out[...] = coupling
     weights_out[...] = dot_t(inverse, coupling)
     for copy in sends:
@@ -319,6 +349,8 @@
     rows, cols = trailing.shape
     half = nc // 2
     piece = width // nr
+    groups = 2 if width % (2 * 8 * nr) == 0 else 1
+    wide = width // groups
     f32 = jnp.float32
     square = jax.ShapeDtypeStruct((width, width), f32)
     tall = jax.ShapeDtypeStruct((width, cols), f32)
@@ -335,11 +367,12 @@
             pltpu.VMEM((nr, piece, width), f32),
             pltpu.VMEM((nc, piece, width), f32),
             pltpu.VMEM((width, width), f32),
-            pltpu.VMEM((width, cols), f32),
-            pltpu.VMEM((nr, piece, cols), f32),
-            pltpu.VMEM((width, cols), f32),
+            pltpu.VMEM((groups, wide, cols), f32),
+            pltpu.VMEM((groups, nr, wide // nr, cols), f32),
+            pltpu.VMEM((groups, wide, cols), f32),
             pltpu.VMEM((width // 2, width // 2), f32),
             pltpu.VMEM((width // 2, width // 2), f32),
+            pltpu.VMEM((width, width), f32),
             dma((2,)),
             dma((CHUNKS,)), dma((CHUNKS,)),
             dma((half,)), dma((half,)),
@@ -347,8 +380,8 @@
             dma((nr,)), dma((nr,)),
             dma((nc,)), dma((nc,)),
             dma((nr,)), dma((nr,)),
-            dma((nr,)), dma((nr,)),
-            dma((nr,)), dma((nr,)),
+            dma((groups, nr)), dma((groups, nr)),
+            dma((groups, nr)), dma((groups, nr)),
         ],
         compiler_params=pltpu.CompilerParams(
             collective_id=0, has_side_effects=True, vmem_limit_bytes=20 * 1024 * 1024

time: 79.5 us -> 76.6 us (0.964)
  Pallas kernels: 78.7 us -> 75.9 us
    pallas_call x1, Pallas kernels: 71.7 us -> 68.8 us  [local(): pl.pallas_call(functools.partial(factor_kernel, nr, nc), out_shape=(jax.S...]
where the time goes in v3:
time: 76.6 us; the launch traced here: 76.5 us
  Pallas kernels  75.9 us (99%)
    pallas_call x1, Pallas kernels, local(): pl.pallas_call(functools.partial(factor_kernel, nr, nc), out_shape=(jax.S...  68.8 us
    pallas_call x1, Pallas kernels, local(): pl.pallas_call(functools.partial(update_kernel, shrink), out_shape=(squar...  7.03 us

profile of v3, /device:TPU:0, one launch (start us, length us, event | category | flops | bytes accessed | tf_op | source)
XLA Modules:
  0.0 76.5 jit_solution(13767118331270641274)
XLA Ops:
  0.6 68.8 %factor.1 = (f32[4,2048,256]{2,1,0:T(8,128)S(1)}, f32[8192,256]{1,0:T(8,128)S(1)}, f32[256,256]{1,0:T(8,128)S(1)}, f32[256,256]{1,0:T(8,128)S(1)}, f32[256,256]{1,0:T(8,128)S(1)}) custom-call(f32[2048,256]{1,0:T(8,128)} %panel.1, f32[8192,256]{1,0:T(8,128)} %trailing.1), custom_call_target="tpu_custom_call" | custom-call | tf_op jit(solution)/shard_map/factor/pallas_call | solution.py:360
  69.5 7.0 %update.1 = (f32[256,256]{1,0:T(8,128)}, f32[256,256]{1,0:T(8,128)}, f32[8192,256]{1,0:T(8,128)}) custom-call(f32[8192,256]{1,0:T(8,128)S(1)} %bitcast.1, f32[8192,256]{1,0:T(8,128)S(1)} %get-tuple-element.9.trailing, f32[256,256]{1,0:T(8,128)S(1)} %get-tuple-element.10.upper, f32[256,256]{1,0:T(8,128)S(1)} %get-tuple-element.11.coupling, ...), custom_call_target="tpu_custom_call" | custom-call | tf_op jit(solution)/shard_map/update/pallas_call | solution.py:393

commit v4 on v3

--- a/solution.py
+++ b/solution.py
@@ -10,8 +10,9 @@
 MESH = pl.DeviceIdType.MESH
 HIGHEST = lax.Precision.HIGHEST
 CHUNKS = 8
-EARLY = 3
-MORE = (1, 1, 1, 0, 1, 0, 1, 0)
+ITEMS = 16
+EARLY = 6
+MORE = (2, 2, 2, 0, 2, 0, 2, 0)
 GROUP = 4
 TILES = 16
 
@@ -82,7 +83,7 @@
 def factor_kernel(
     nr, nc,
     panel, trailing, block, trail, upper_out, coupling_out, weights_out,
-    gram, gram_stage, col_stage, gram_sum, cross, cross_stage, cross_sum, work, minv, inv,
+    gram, gram_stage, col_stage, gram_sum, cross, cross_stage, cross_sum, work, minv, inv, square,
     load_sem, y_send, y_recv, half_send, half_recv, fwd_send, fwd_recv,
     rs_send, rs_recv, cx_send, cx_recv, ag_send, ag_recv, xrs_send, xrs_recv, xag_send, xag_recv,
 ):
@@ -94,7 +95,7 @@
     chunk = depth // CHUNKS
     piece = width // nr
     groups = cross.shape[0]
-    per_group = CHUNKS // groups
+    per_group = ITEMS // groups
     deep = depth // per_group
     wide = width // groups
     cross_piece = wide // nr
@@ -203,7 +204,7 @@
         remote(col_stage.at[me_c], col_stage.at[me_c], cx_send.at[d], cx_recv.at[d], {"cols": lax.rem(me_c + d, nc)})
         for d in range(1, nc)
     ]
-    for k in range(EARLY, CHUNKS):
+    for k in range(EARLY, ITEMS):
         send_across(k)
     for d in range(1, half):
         half_copies[d - 1].wait_recv()
@@ -223,7 +224,7 @@
         rows, lanes = item(k)
         for d in range(1, half):
             peer = side * half + lax.rem(place + d, half)
-            slot = (d - 1) * CHUNKS + k
+            slot = (d - 1) * ITEMS + k
             part = block.at[across, rows, lanes]
             forwards[d, k] = remote(part, part, fwd_send.at[slot], fwd_recv.at[slot], {"cols": peer})
         add_item(across, k)
@@ -245,13 +246,13 @@
         cross_ag[g] = gather(cross_sum.at[g], xag_send.at[g], xag_recv.at[g], cross_piece)
 
     pending = []
-    for k in range(CHUNKS):
-        pending.append([functools.partial(take, k)] + ([functools.partial(take_forward, k - 1)] if k % per_group else []))
+    for k in range(ITEMS):
+        pending.append(([functools.partial(take_forward, k - 1)] if k % per_group else []) + [functools.partial(take, k)])
         if k % per_group == per_group - 1:
             pending[-1].append(functools.partial(take_forward, k))
             pending[-1].append(functools.partial(start_cross, k // per_group))
     for g in range(groups - 1):
-        pending[(g + 1) * per_group + 1].append(functools.partial(share_cross, g))
+        pending[(g + 1) * per_group + 2].append(functools.partial(share_cross, g))
 
     def advance():
         for task in pending.pop(0):
@@ -259,7 +260,7 @@
 
     def run(first, last, more):
         eliminate(work, minv, first, last)
-        if more:
+        for _ in range(more):
             advance()
 
     for _ in range(EARLY):
@@ -289,13 +290,21 @@
     inv[pl.ds(hw, hw), pl.ds(hw, hw)] = inverse2
     while pending:
         advance()
+    inverse = inv[...]
+    square[...] = dot_t(inverse, inverse)
+    last = slice((groups - 1) * wide, groups * wide)
+    coupling_out[...] = jnp.zeros_like(coupling_out)
+    weights_out[...] = jnp.zeros_like(weights_out)
+    for g in range(groups - 1):
+        arrived(cross_ag[g])
+        part = cross_sum[g]
+        coupling_out[...] += dot(inv[:, g * wide : (g + 1) * wide], part)
+        weights_out[...] += dot(square[:, g * wide : (g + 1) * wide], part)
     share_cross(groups - 1)
-    for g in range(groups):
-        arrived(cross_ag[g])
-    inverse = inv[...]
-    coupling = dot(inverse, jnp.concatenate([cross_sum[g] for g in range(groups)], axis=0))
-    coupling_out[...] = coupling
-    weights_out[...] = dot_t(inverse, coupling)
+    arrived(cross_ag[groups - 1])
+    part = cross_sum[groups - 1]
+    weights_out[...] += dot(square[:, last], part)
+    coupling_out[...] += dot(inv[:, last], part)
     for copy in sends:
         copy.wait_send()
 
@@ -373,10 +382,11 @@
             pltpu.VMEM((width // 2, width // 2), f32),
             pltpu.VMEM((width // 2, width // 2), f32),
             pltpu.VMEM((width, width), f32),
+            pltpu.VMEM((width, width), f32),
             dma((2,)),
-            dma((CHUNKS,)), dma((CHUNKS,)),
+            dma((ITEMS,)), dma((ITEMS,)),
             dma((half,)), dma((half,)),
-            dma((CHUNKS * half,)), dma((CHUNKS * half,)),
+            dma((ITEMS * half,)), dma((ITEMS * half,)),
             dma((nr,)), dma((nr,)),
             dma((nc,)), dma((nc,)),
             dma((nr,)), dma((nr,)),

time: 76.6 us -> 77.7 us (1.014)
  Pallas kernels: 75.9 us -> 76.9 us
    pallas_call x1, Pallas kernels: 68.8 us -> 69.9 us  [local(): pl.pallas_call(functools.partial(factor_kernel, nr, nc), out_shape=(jax.S...]
where the time goes in v4:
time: 77.7 us; the launch traced here: 77.6 us
  Pallas kernels  76.9 us (99%)
    pallas_call x1, Pallas kernels, local(): pl.pallas_call(functools.partial(factor_kernel, nr, nc), out_shape=(jax.S...  69.9 us
    pallas_call x1, Pallas kernels, local(): pl.pallas_call(functools.partial(update_kernel, shrink), out_shape=(squar...  7.03 us

profile of v4, /device:TPU:0, one launch (start us, length us, event | category | flops | bytes accessed | tf_op | source)
XLA Modules:
  0.0 77.6 jit_solution(18007550505858044854)
XLA Ops:
  0.6 69.9 %factor.1 = (f32[4,2048,256]{2,1,0:T(8,128)S(1)}, f32[8192,256]{1,0:T(8,128)S(1)}, f32[256,256]{1,0:T(8,128)S(1)}, f32[256,256]{1,0:T(8,128)S(1)}, f32[256,256]{1,0:T(8,128)S(1)}) custom-call(f32[2048,256]{1,0:T(8,128)} %panel.1, f32[8192,256]{1,0:T(8,128)} %trailing.1), custom_call_target="tpu_custom_call" | custom-call | tf_op jit(solution)/shard_map/factor/pallas_call | solution.py:369
  70.6 7.0 %update.1 = (f32[256,256]{1,0:T(8,128)}, f32[256,256]{1,0:T(8,128)}, f32[8192,256]{1,0:T(8,128)}) custom-call(f32[8192,256]{1,0:T(8,128)S(1)} %bitcast.1, f32[8192,256]{1,0:T(8,128)S(1)} %get-tuple-element.9.trailing, f32[256,256]{1,0:T(8,128)S(1)} %get-tuple-element.10.upper, f32[256,256]{1,0:T(8,128)S(1)} %get-tuple-element.11.coupling, ...), custom_call_target="tpu_custom_call" | custom-call | tf_op jit(solution)/shard_map/update/pallas_call | solution.py:403

commit v5 on v4

--- a/solution.py
+++ b/solution.py
@@ -10,11 +10,11 @@
 MESH = pl.DeviceIdType.MESH
 HIGHEST = lax.Precision.HIGHEST
 CHUNKS = 8
-ITEMS = 16
-EARLY = 6
-MORE = (2, 2, 2, 0, 2, 0, 2, 0)
+ITEMS = 8
+EARLY = 3
+MORE = (1, 1, 1, 0, 1, 0, 1, 0)
 GROUP = 4
-TILES = 16
+TILES = 8
 
 
 def dot(left, right):

time: 77.7 us -> 74.3 us (0.956)
  Pallas kernels: 76.9 us -> 73.5 us
    pallas_call x1, Pallas kernels: 69.9 us -> 67.7 us  [local(): pl.pallas_call(functools.partial(factor_kernel, nr, nc), out_shape=(jax.S...]
    pallas_call x1, Pallas kernels: 7.03 us -> 5.82 us  [local(): pl.pallas_call(functools.partial(update_kernel, shrink), out_shape=(squar...]
where the time goes in v5:
time: 74.3 us; the launch traced here: 74.2 us
  Pallas kernels  73.5 us (99%)
    pallas_call x1, Pallas kernels, local(): pl.pallas_call(functools.partial(factor_kernel, nr, nc), out_shape=(jax.S...  67.7 us
    pallas_call x1, Pallas kernels, local(): pl.pallas_call(functools.partial(update_kernel, shrink), out_shape=(squar...  5.82 us

profile of v5, /device:TPU:0, one launch (start us, length us, event | category | flops | bytes accessed | tf_op | source)
XLA Modules:
  0.0 74.2 jit_solution(5898509377918346415)
XLA Ops:
  0.6 67.7 %factor.1 = (f32[4,2048,256]{2,1,0:T(8,128)S(1)}, f32[8192,256]{1,0:T(8,128)S(1)}, f32[256,256]{1,0:T(8,128)S(1)}, f32[256,256]{1,0:T(8,128)S(1)}, f32[256,256]{1,0:T(8,128)S(1)}) custom-call(f32[2048,256]{1,0:T(8,128)} %panel.1, f32[8192,256]{1,0:T(8,128)} %trailing.1), custom_call_target="tpu_custom_call" | custom-call | tf_op jit(solution)/shard_map/factor/pallas_call | solution.py:369
  68.3 5.8 %update.1 = (f32[256,256]{1,0:T(8,128)}, f32[256,256]{1,0:T(8,128)}, f32[8192,256]{1,0:T(8,128)}) custom-call(f32[8192,256]{1,0:T(8,128)S(1)} %bitcast.1, f32[8192,256]{1,0:T(8,128)S(1)} %get-tuple-element.9.trailing, f32[256,256]{1,0:T(8,128)S(1)} %get-tuple-element.10.upper, f32[256,256]{1,0:T(8,128)S(1)} %get-tuple-element.11.coupling, ...), custom_call_target="tpu_custom_call" | custom-call | tf_op jit(solution)/shard_map/update/pallas_call | solution.py:403
